TPU v7x, 512 devices: a whole 4x8x8 slice. The times are simulated.
512 devices in a mesh: leaf: 8 (over z), row: 8 (over y), col: 8 (over x, core).
Axes of the slice: x: 4, y: 8, z: 8, core: 2. Of those that a mesh axis runs over, the one named last changes fastest.
Arguments:
- child_inverse: bfloat16 [8, 2, 3072, 3072], P('leaf', None, 'row', 'col'), as said below
- child_rhs: bfloat16 [8, 2, 3072, 256], P('leaf', None, 'col'), may hold values from -6 to 6
- child_to_mid: bfloat16 [8, 2, 2048, 3072], P('leaf', None, ('row', 'col')), may hold values from -0.109375 to 0.109375
- child_to_root: bfloat16 [8, 2, 2048, 3072], P('leaf', None, ('row', 'col')), may hold values from -0.109375 to 0.109375
- mid_rows_list: int32 [8, 2, 2048], P('leaf'), may hold values from 0 to 4095, as said below
- root_rows_list: int32 [8, 2, 2048], P('leaf'), may hold values from 0 to 8191, as said below
- mid_inverse: bfloat16 [8, 4096, 4096], P('leaf', 'row', 'col'), as said below
- mid_rhs: bfloat16 [8, 4096, 256], P('leaf', 'col'), may hold values from -6 to 6
- mid_to_root: bfloat16 [8, 2048, 4096], P('leaf', ('row', 'col')), may hold values from -0.09375 to 0.09375
- mid_root_list: int32 [8, 2048], P('leaf'), may hold values from 0 to 8191, as said below
- root_inverse: bfloat16 [8192, 8192], P(('leaf', 'row'), 'col'), as said below
- root_rhs: bfloat16 [8192, 256], P('col'), may hold values from -6 to 6
Outputs:
- child_solution: bfloat16 [8, 2, 3072, 256], P('leaf', None, 'row')
- mid_solution: bfloat16 [8, 4096, 256], P('leaf', 'row')
- root_solution: bfloat16 [8192, 256], P(('leaf', 'row'))
Inputs may be any that keep to these rules, and one draw needn't show every extreme that they name: `mid_rows_list`: each list of a child holds 2048 distinct rows of its middle supernode in increasing order, always with the first and the last. `root_rows_list`: each list of a child holds 2048 distinct rows of the root in increasing order, always with the first and the last. `mid_root_list`: each list holds 2048 distinct rows of the root in increasing order, always with the first and the last. `child_inverse`: lower triangular with a positive diagonal. `mid_inverse`: lower triangular with a positive diagonal. `root_inverse`: lower triangular with a positive diagonal.
All inputs are finite; a program needn't handle non-finite values.
Results may differ from a plain program's by a relative error of at most 0.0085.
Values may be sent and summed in bfloat16 or wider, within the bound.
A program may use at most 64 MiB of HBM per device.

v0:
```python
import jax
import jax.numpy as jnp
from jax import lax
from jax.sharding import PartitionSpec as P


def solve_spread(partial_value):
    placed = lax.psum(partial_value, "col").astype(jnp.bfloat16)
    whole_rows = lax.all_gather(placed, "row", axis=2, tiled=True)
    return (placed, whole_rows)


def gather_updates(pieces):
    return lax.all_gather(pieces, ("row", "col"), axis=2, tiled=True)


def scatter_block(values, rows_list, piece_rows, col_index):
    width = values.shape[-1]
    flat_values = values.reshape(-1, width).astype(jnp.float32)
    offsets = rows_list.reshape(-1) - col_index * piece_rows
    inside = (offsets >= 0) & (offsets < piece_rows)
    target = jnp.where(inside, offsets, piece_rows)
    summed = jnp.zeros((piece_rows + 1, width), jnp.float32).at[target].add(flat_values)
    return summed[:piece_rows]


def per_device(
    child_inverse,
    child_rhs,
    child_to_mid,
    child_to_root,
    mid_rows_list,
    root_rows_list,
    mid_inverse,
    mid_rhs,
    mid_to_root,
    mid_root_list,
    root_inverse,
    root_rhs,
):
    grid_size = lax.axis_size("row") * lax.axis_size("col")
    col_index = lax.axis_index("col")
    rhs_width = child_rhs.shape[3]
    child_partial = jnp.einsum(
        "gcij,gcjr->gcir", child_inverse, child_rhs, preferred_element_type=jnp.float32
    )
    child_local, child_whole = solve_spread(child_partial)
    mid_piece = child_to_mid.shape[2]
    root_piece = child_to_root.shape[2]
    update_mid = jnp.einsum(
        "gcuj,gcjr->gcur", child_to_mid, child_whole, preferred_element_type=jnp.float32
    ).astype(jnp.bfloat16)
    update_root = jnp.einsum(
        "gcuj,gcjr->gcur", child_to_root, child_whole, preferred_element_type=jnp.float32
    ).astype(jnp.bfloat16)
    stacked = jnp.concatenate((update_mid, update_root), axis=2)
    gathered = gather_updates(stacked)
    lead_count = gathered.shape[0]
    child_count = gathered.shape[1]
    split_view = gathered.reshape(
        lead_count, child_count, grid_size, mid_piece + root_piece, rhs_width
    )
    mid_updates = split_view[:, :, :, :mid_piece].reshape(
        lead_count, child_count, grid_size * mid_piece, rhs_width
    )
    root_updates = split_view[:, :, :, mid_piece:].reshape(
        lead_count, child_count, grid_size * root_piece, rhs_width
    )
    root_group = root_rhs.shape[0]
    child_root_term = scatter_block(root_updates, root_rows_list, root_group, col_index)
    mid_term = scatter_block(mid_updates, mid_rows_list, mid_rhs.shape[1], col_index)
    mid_input = (mid_rhs[0].astype(jnp.float32) - mid_term).astype(jnp.bfloat16)
    mid_partial = jnp.dot(mid_inverse[0], mid_input, preferred_element_type=jnp.float32)[None, None]
    mid_local, mid_whole = solve_spread(mid_partial)
    update_top = jnp.dot(
        mid_to_root[0], mid_whole[0, 0], preferred_element_type=jnp.float32
    ).astype(jnp.bfloat16)[None, None]
    top_whole = gather_updates(update_top)
    top_term = scatter_block(top_whole, mid_root_list, root_group, col_index)
    root_sum = lax.psum(child_root_term + top_term, "leaf")
    root_input = (root_rhs.astype(jnp.float32) - root_sum).astype(jnp.bfloat16)
    root_partial = jnp.dot(root_inverse, root_input, preferred_element_type=jnp.float32)
    root_solution = lax.psum(root_partial, "col").astype(jnp.bfloat16)
    return (child_local, mid_local[0], root_solution)


def solution(mesh):
    in_specs = (
        P("leaf", None, "row", "col"),
        P("leaf", None, "col", None),
        P("leaf", None, ("row", "col"), None),
        P("leaf", None, ("row", "col"), None),
        P("leaf", None, None),
        P("leaf", None, None),
        P("leaf", "row", "col"),
        P("leaf", "col", None),
        P("leaf", ("row", "col"), None),
        P("leaf", None),
        P(("leaf", "row"), "col"),
        P("col", None),
    )
    out_specs = (P("leaf", None, "row", None), P("leaf", "row", None), P(("leaf", "row"), None))
    return jax.shard_map(
        per_device, mesh=mesh, in_specs=in_specs, out_specs=out_specs, check_vma=False
    )
```

profile of v0, /device:TPU:8, one launch (start us, length us, event | category | flops | bytes accessed | tf_op | source)
XLA Modules:
  0.0 500.9 jit_solution(5121878186767649496)
XLA Ops:
  7.2 1.0 copy-done
  8.2 1.4 convolution_bitcast_fusion
  9.6 32.4 %all-reduce.6 = bf16[1,2,384,256]{3,2,1,0:T(8,128)(2,1)} all-reduce(f32[1,2,384,256]{3,2,1,0:T(8,128)S(1)} %convolution_bitcast_fusion), channel_id=1, replica_groups=mesh['leaf'=8,'row'=8,'col'=8] {'col'}, use_global_device_ids=true, to_apply=%region_0.0 | all-reduce | flops 196608 | bytes 1179648 | tf_op jit(solution)/shard_map/psum | solution.py:8
  42.1 49.2 %all-gather.6.cloned.1.call-done = bf16[1,2,3072,256]{3,2,1,0:T(8,128)(2,1)} async-done(((bf16[1,2,384,256]{3,2,1,0:T(8,128)(2,1)}), bf16[1,2,3072,256]{3,2,1,0:T(8,128)(2,1)}) %all-gather.6.cloned.1.call-update) | async-done | bytes 3145744 | tf_op jit(solution)/shard_map/all_gather | solution.py:9
  91.3 2.7 fusion.18
  94.0 0.1 copy-done.1
  94.1 0.6 fusion.21
  94.8 0.6 pad_maximum_fusion
  95.6 82.8 %all-gather.8.cloned.1.call-done = bf16[1,2,4096,256]{3,2,1,0:T(8,128)(2,1)} async-done(((bf16[1,2,64,256]{3,2,1,0:T(8,128)(2,1)}), bf16[1,2,4096,256]{3,2,1,0:T(8,128)(2,1)}) %all-gather.8.cloned.1.call-update) | async-done | bytes 4194320 | tf_op jit(solution)/shard_map/all_gather | solution.py:14
  178.4 4.2 fusion.42
  182.6 28.5 %scatter_custom_fusion = f32[513,256]{1,0:T(8,128)S(1)} fusion(s32[4096]{0:T(1024)S(1)} %bitcast.88, bf16[4096,256]{1,0:T(8,128)(2,1)} %bitcast.83, f32[]{:T(128)} %constant.7.clone.1), kind=kCustom, calls=%fused_computation.5 | custom fusion | flops 2097152 | bytes 2622468 | tf_op jit(solution)/shard_map/scatter-add | solution.py:23
  211.2 2.2 convolution_bitcast_fusion.1
  213.4 32.1 %all-reduce.7 = bf16[1,1,512,256]{2,3,1,0:T(8,128)(2,1)} all-reduce(f32[1,1,512,256]{2,3,1,0:T(8,128)} %convolution_bitcast_fusion.1), channel_id=1, replica_groups=mesh['leaf'=8,'row'=8,'col'=8] {'col'}, use_global_device_ids=true, to_apply=%region_2.3 | all-reduce | flops 131072 | bytes 786432 | tf_op jit(solution)/shard_map/psum | solution.py:8
  245.5 40.1 %all-gather.10.cloned.1.call-done = bf16[1,1,4096,256]{2,3,1,0:T(8,128)(2,1)} async-done(((bf16[1,1,512,256]{2,3,1,0:T(8,128)(2,1)}), bf16[1,1,4096,256]{2,3,1,0:T(8,128)(2,1)}) %all-gather.10.cloned.1.call-update) | async-done | bytes 2097168 | tf_op jit(solution)/shard_map/all_gather | solution.py:9
  285.7 2.9 fusion.27
  288.8 29.2 %scatter_custom_fusion.1 = f32[1025,256]{1,0:T(8,128)} fusion(s32[4096]{0:T(1024)S(1)} %bitcast.89, bf16[4096,256]{1,0:T(8,128)(2,1)S(1)} %bitcast.82, f32[]{:T(128)} %constant.7.clone.1), kind=kCustom, calls=%fused_computation.3 | custom fusion | flops 2097152 | bytes 3146756 | tf_op jit(solution)/shard_map/scatter-add | solution.py:23
  318.0 51.5 %all-gather.12.cloned.1.call-done = bf16[2048,256]{1,0:T(8,128)(2,1)} async-done(((bf16[32,256]{1,0:T(8,128)(2,1)}), bf16[2048,256]{1,0:T(8,128)(2,1)}) %all-gather.12.cloned.1.call-update) | async-done | bytes 1048592 | tf_op jit(solution)/shard_map/all_gather | solution.py:14
  369.5 14.9 %scatter_custom_fusion.2 = f32[1025,256]{1,0:T(8,128)S(1)} fusion(s32[2048]{0:T(1024)S(1)} %bitcast.90, bf16[2048,256]{1,0:T(8,128)(2,1)} %all-gather.12.cloned.1.call-done, f32[]{:T(128)} %constant.7.clone.1), kind=kCustom, calls=%fused_computation.13 | custom fusion | flops 1048576 | bytes 2098180 | tf_op jit(solution)/shard_map/scatter-add | solution.py:23
  384.4 1.2 slice_add_fusion
  385.6 0.8 copy.17
  386.5 80.8 %all-reduce.5.cloned.1.call-done = f32[1024,256]{1,0:T(8,128)} async-done(((f32[1024,256]{1,0:T(8,128)}), f32[1024,256]{1,0:T(8,128)}) %all-reduce.5.cloned.1.call-update) | async-done | bytes 1048592 | tf_op jit(solution)/shard_map/psum | solution.py:80
  467.3 1.6 convolution_bitcast_fusion.2
  468.9 24.7 %all-reduce.8 = bf16[128,256]{0,1:T(8,128)(2,1)S(1)} all-reduce(f32[128,256]{0,1:T(8,128)S(1)} %convolution_bitcast_fusion.2), channel_id=1, replica_groups=mesh['leaf'=8,'row'=8,'col'=8] {'col'}, use_global_device_ids=true, to_apply=%region_6.7 | all-reduce | flops 32768 | bytes 196608 | tf_op jit(solution)/shard_map/psum | solution.py:83
  493.6 0.7 copy.18
  (37 shorter events, 0.5 us)
Async XLA Ops:
  7.2 1.1 copy-start
  7.2 84.1 %copy-start.5 = (bf16[1,2,32,3072]{3,2,1,0:T(8,128)(2,1)S(1)}, bf16[1,2,32,3072]{3,2,1,0:T(8,128)(2,1)}, u32[]{:S(2)}) copy-start(bf16[1,2,32,3072]{3,2,1,0:T(8,128)(2,1)} %param.14) | copy-start | bytes 1179652
  7.2 84.1 %all-gather.6.cloned.1.call-start = ((), (), s32[]{:S(2)}) async-start(), calls=%async_computation | async-start | bytes 3538944 | tf_op jit(solution)/shard_map/all_gather | solution.py:9
  42.0 52.0 %copy-start.6 = (bf16[1,2,32,3072]{3,2,1,0:T(8,128)(2,1)S(1)}, bf16[1,2,32,3072]{3,2,1,0:T(8,128)(2,1)}, u32[]{:S(2)}) copy-start(bf16[1,2,32,3072]{3,2,1,0:T(8,128)(2,1)} %param.15) | copy-start | bytes 1179652
  42.0 136.4 %all-gather.8.cloned.1.call-start = ((), (), s32[]{:S(2)}) async-start(), calls=%async_computation.1 | async-start | bytes 4259840 | tf_op jit(solution)/shard_map/all_gather | solution.py:14
  91.3 2.8 copy-start.1
  94.1 1.4 copy-start.8
  95.5 190.2 %all-gather.10.cloned.1.call-start = ((), (), s32[]{:S(2)}) async-start(), calls=%async_computation.2 | async-start | bytes 2359296 | tf_op jit(solution)/shard_map/all_gather | solution.py:9
  182.6 28.5 %copy-start.7 = (bf16[1,512,256]{2,1,0:T(8,128)(2,1)S(1)}, bf16[1,512,256]{2,1,0:T(8,128)(2,1)}, u32[]{:S(2)}) copy-start(bf16[1,512,256]{2,1,0:T(8,128)(2,1)} %param.19) | copy-start | bytes 786436
  213.4 75.3 %copy-start.9 = (s32[1,2,2048]{2,1,0:T(2,128)S(1)}, s32[1,2,2048]{2,1,0:T(2,128)}, u32[]{:S(2)}) copy-start(s32[1,2,2048]{2,1,0:T(2,128)} %param.17) | copy-start | bytes 49156
  213.4 75.4 %copy-start.10 = (s32[1,2048]{1,0:T(1,128)S(1)}, s32[1,2048]{1,0:T(1,128)}, u32[]{:S(2)}) copy-start(s32[1,2048]{1,0:T(1,128)} %param.21) | copy-start | bytes 24580
  245.5 124.1 %all-gather.12.cloned.1.call-start = ((), (), s32[]{:S(2)}) async-start(), calls=%async_computation.4 | async-start | bytes 1064960 | tf_op jit(solution)/shard_map/all_gather | solution.py:14
  288.6 178.7 %all-reduce.5.cloned.1.call-start = ((), (), s32[]{:S(2)}) async-start(), calls=%async_computation.3 | async-start | bytes 2097152 | tf_op jit(solution)/shard_map/psum | solution.py:80
  318.0 66.4 %copy-start.2 = (f32[1025,256]{1,0:T(8,128)S(1)}, f32[1025,256]{1,0:T(8,128)}, u32[]{:S(2)}) copy-start(f32[1025,256]{1,0:T(8,128)} %scatter_custom_fusion.1) | copy-start | bytes 3148804
  384.4 1.2 copy-start.3
  384.4 82.9 %copy-start.4 = (bf16[1024,256]{1,0:T(8,128)(2,1)S(1)}, bf16[1024,256]{1,0:T(8,128)(2,1)}, u32[]{:S(2)}) copy-start(bf16[1024,256]{1,0:T(8,128)(2,1)} %param.23) | copy-start | bytes 1572868
Sparse Core Ops, SparseCore 0:
  42.2 49.0 all-gather.5
  95.6 82.8 all-gather.7
  245.6 40.0 all-gather.9
  289.4 80.0 all-gather.11
  385.8 81.4 all-reduce.4
where the time goes:
time: 501 us
  waiting for transfers between devices  305 us (61%)
  blocking collectives  89.2 us (18%)
  other arithmetic  74.5 us (15%)
  between operations  14 us (3%)
  matrix products  11.4 us (2%)
  local copies, waits for them, and re-layouts  7.04 us (1%)
    all_gather x2, waiting for transfers between devices, gather_updates(): return lax.all_gather(pieces, ('row', 'col'), axis=2, tiled=True)  134 us
    all_gather x2, waiting for transfers between devices, solve_spread(): whole_rows = lax.all_gather(placed, 'row', axis=2, tiled=True)  89.3 us
    psum x1, waiting for transfers between devices, per_device(): root_sum = lax.psum(child_root_term + top_term, 'leaf')  80.8 us
    scatter-add x3, other arithmetic, scatter_block(): jnp.zeros((piece_rows + 1, width), jnp.float32).at[target].add(flat_values)  72.6 us
    psum x2, blocking collectives, solve_spread(): placed = lax.psum(partial_value, 'col').astype(jnp.bfloat16)  64.5 us
    psum x1, blocking collectives, per_device(): root_solution = lax.psum(root_partial, 'col').astype(jnp.bfloat16)  24.7 us
  transfers between devices with their start and end apart: 5, of which 5 were waited for; matrix products, arithmetic and copies ran while one was open for 6% of the time, Pallas kernels for 0%

commit v1 on v0

--- a/solution.py
+++ b/solution.py
@@ -11,7 +11,10 @@
 
 
 def gather_updates(pieces):
-    return lax.all_gather(pieces, ("row", "col"), axis=2, tiled=True)
+    return jnp.concatenate(
+        lax.all_to_all(jnp.stack([pieces] * lax.axis_size(("row", "col"))), ("row", "col"), 0, 0),
+        axis=2,
+    )
 
 
 def scatter_block(values, rows_list, piece_rows, col_index):

time: 501 us -> 482 us (0.962)
  waiting for transfers between devices: 305 us -> 266 us
  starting transfers between devices: 0.2 us -> 16.9 us
    all_gather x2 -> x0, waiting for transfers between devices: 134 us -> none  [gather_updates(): return lax.all_gather(pieces, ('row', 'col'), axis=2, tiled=True)]
    all_to_all x0 -> x2, waiting for transfers between devices: none -> 95.1 us  [gather_updates(): lax.all_to_all(jnp.stack([pieces] * lax.axis_size(('row', 'col'))), ('row...]
    all_to_all x0 -> x2, starting transfers between devices: none -> 16.8 us  [gather_updates(): lax.all_to_all(jnp.stack([pieces] * lax.axis_size(('row', 'col'))), ('row...]
  transfers between devices with their start and end apart: 5 -> 5, of which waited for: 5 -> 4; matrix products, arithmetic and copies ran while one was open for 6% -> 6% of each run, Pallas kernels for 0% -> 0%
where the time goes in v1:
time: 482 us
  waiting for transfers between devices  266 us (55%)
  blocking collectives  89.5 us (19%)
  other arithmetic  73.9 us (15%)
  starting transfers between devices  16.9 us (4%)
  between operations  14 us (3%)
  matrix products  10.8 us (2%)
  local copies, waits for them, and re-layouts  10.7 us (2%)
    all_to_all x2, waiting for transfers between devices, gather_updates(): lax.all_to_all(jnp.stack([pieces] * lax.axis_size(('row', 'col'))), ('row...  95.1 us
    all_gather x2, waiting for transfers between devices, solve_spread(): whole_rows = lax.all_gather(placed, 'row', axis=2, tiled=True)  87.6 us
    psum x1, waiting for transfers between devices, per_device(): root_sum = lax.psum(child_root_term + top_term, 'leaf')  83.2 us
    scatter-add x3, other arithmetic, scatter_block(): jnp.zeros((piece_rows + 1, width), jnp.float32).at[target].add(flat_values)  72.6 us
    psum x2, blocking collectives, solve_spread(): placed = lax.psum(partial_value, 'col').astype(jnp.bfloat16)  64.8 us
    psum x1, blocking collectives, per_device(): root_solution = lax.psum(root_partial, 'col').astype(jnp.bfloat16)  24.7 us
    all_to_all x2, starting transfers between devices, gather_updates(): lax.all_to_all(jnp.stack([pieces] * lax.axis_size(('row', 'col'))), ('row...  16.8 us
  transfers between devices with their start and end apart: 5, of which 4 were waited for; matrix products, arithmetic and copies ran while one was open for 6% of the time, Pallas kernels for 0%

profile of v1, /device:TPU:8, one launch (start us, length us, event | category | flops | bytes accessed | tf_op | source)
XLA Modules:
  0.0 481.8 jit_solution(18130020414846556612)
XLA Ops:
  7.2 1.0 copy-done
  8.2 1.4 convolution_bitcast_fusion
  9.6 32.4 %all-reduce.6 = bf16[1,2,384,256]{3,2,1,0:T(8,128)(2,1)} all-reduce(f32[1,2,384,256]{3,2,1,0:T(8,128)S(1)} %convolution_bitcast_fusion), channel_id=1, replica_groups=mesh['leaf'=8,'row'=8,'col'=8] {'col'}, use_global_device_ids=true, to_apply=%region_0.0 | all-reduce | flops 196608 | bytes 1179648 | tf_op jit(solution)/shard_map/psum | solution.py:8
  42.0 49.3 %all-gather.3.cloned.1.call-done = bf16[1,2,3072,256]{3,2,1,0:T(8,128)(2,1)} async-done(((bf16[1,2,384,256]{3,2,1,0:T(8,128)(2,1)}), bf16[1,2,3072,256]{3,2,1,0:T(8,128)(2,1)}) %all-gather.3.cloned.1.call-update) | async-done | bytes 3145744 | tf_op jit(solution)/shard_map/all_gather | solution.py:9
  91.3 2.7 fusion.18
  94.8 2.5 stack.4
  97.3 8.7 %all-to-all-start = ((bf16[64,1,2,64,256]{4,3,2,1,0:T(8,128)(2,1)}), bf16[64,1,2,64,256]{4,3,2,1,0:T(8,128)(2,1)}, u32[]{:S(2)}, u32[]{:S(2)}) async-start(bf16[64,1,2,64,256]{4,3,2,1,0:T(8,128)(2,1)} %stack.4), calls=%async_computation | async-start | bytes 8388608 | tf_op jit(solution)/shard_map/all_to_all | solution.py:15
  106.1 95.1 %all-to-all-done = bf16[64,1,2,64,256]{4,3,2,1,0:T(8,128)(2,1)} async-done(((bf16[64,1,2,64,256]{4,3,2,1,0:T(8,128)(2,1)}), bf16[64,1,2,64,256]{4,3,2,1,0:T(8,128)(2,1)}, u32[]{:S(2)}, u32[]{:S(2)}) %all-to-all-start) | async-done | bytes 4194336 | tf_op jit(solution)/shard_map/all_to_all | solution.py:15
  201.2 2.5 copy.27
  203.7 1.8 fusion.42
  205.5 28.5 %scatter_custom_fusion = f32[513,256]{1,0:T(8,128)S(1)} fusion(s32[4096]{0:T(1024)S(1)} %bitcast.94, bf16[4096,256]{1,0:T(8,128)(2,1)} %bitcast.90, f32[]{:T(128)} %constant.7.clone.1), kind=kCustom, calls=%fused_computation.5 | custom fusion | flops 2097152 | bytes 2622468 | tf_op jit(solution)/shard_map/scatter-add | solution.py:26
  234.0 2.2 convolution_bitcast_fusion.1
  236.2 32.4 %all-reduce.7 = bf16[1,1,512,256]{2,3,1,0:T(8,128)(2,1)} all-reduce(f32[1,1,512,256]{2,3,1,0:T(8,128)} %convolution_bitcast_fusion.1), channel_id=1, replica_groups=mesh['leaf'=8,'row'=8,'col'=8] {'col'}, use_global_device_ids=true, to_apply=%region_2.3 | all-reduce | flops 131072 | bytes 786432 | tf_op jit(solution)/shard_map/psum | solution.py:8
  268.6 38.3 %all-gather.5.cloned.1.call-done = bf16[1,1,4096,256]{2,3,1,0:T(8,128)(2,1)} async-done(((bf16[1,1,512,256]{2,3,1,0:T(8,128)(2,1)}), bf16[1,1,4096,256]{2,3,1,0:T(8,128)(2,1)}) %all-gather.5.cloned.1.call-update) | async-done | bytes 2097168 | tf_op jit(solution)/shard_map/all_gather | solution.py:9
  306.9 2.3 fusion.27
  309.3 1.1 stack.5
  310.4 8.1 %all-to-all-start.1 = ((bf16[64,1,1,32,256]{4,3,2,1,0:T(8,128)(2,1)}), bf16[64,1,1,32,256]{4,3,2,1,0:T(8,128)(2,1)}, u32[]{:S(2)}, u32[]{:S(2)}) async-start(bf16[64,1,1,32,256]{4,3,2,1,0:T(8,128)(2,1)} %stack.5), calls=%async_computation.1 | async-start | bytes 2097152 | tf_op jit(solution)/shard_map/all_to_all | solution.py:15
  318.7 29.2 %scatter_custom_fusion.1 = f32[1025,256]{1,0:T(8,128)} fusion(s32[4096]{0:T(1024)S(1)} %bitcast.95, bf16[4096,256]{1,0:T(8,128)(2,1)S(1)} %bitcast.89, f32[]{:T(128)} %constant.7.clone.1), kind=kCustom, calls=%fused_computation.3 | custom fusion | flops 2097152 | bytes 3146756 | tf_op jit(solution)/shard_map/scatter-add | solution.py:26
  348.0 14.9 %scatter_custom_fusion.2 = f32[1025,256]{1,0:T(8,128)S(1)} fusion(s32[2048]{0:T(1024)S(1)} %bitcast.96, bf16[2048,256]{1,0:T(8,128)(2,1)} %bitcast.34, f32[]{:T(128)} %constant.7.clone.1), kind=kCustom, calls=%fused_computation.12 | custom fusion | flops 1048576 | bytes 2098180 | tf_op jit(solution)/shard_map/scatter-add | solution.py:26
  362.9 1.1 slice_add_fusion
  364.1 0.8 copy.22
  364.9 83.2 %all-reduce.5.cloned.1.call-done = f32[1024,256]{1,0:T(8,128)} async-done(((f32[1024,256]{1,0:T(8,128)}), f32[1024,256]{1,0:T(8,128)}) %all-reduce.5.cloned.1.call-update) | async-done | bytes 1048592 | tf_op jit(solution)/shard_map/psum | solution.py:83
  448.1 1.6 convolution_bitcast_fusion.2
  449.8 24.7 %all-reduce.8 = bf16[128,256]{0,1:T(8,128)(2,1)S(1)} all-reduce(f32[128,256]{0,1:T(8,128)S(1)} %convolution_bitcast_fusion.2), channel_id=1, replica_groups=mesh['leaf'=8,'row'=8,'col'=8] {'col'}, use_global_device_ids=true, to_apply=%region_6.7 | all-reduce | flops 32768 | bytes 196608 | tf_op jit(solution)/shard_map/psum | solution.py:86
  (38 shorter events, 1.9 us)
Async XLA Ops:
  7.2 1.1 copy-start
  7.2 84.1 %copy-start.5 = (bf16[1,2,32,3072]{3,2,1,0:T(8,128)(2,1)S(1)}, bf16[1,2,32,3072]{3,2,1,0:T(8,128)(2,1)}, u32[]{:S(2)}) copy-start(bf16[1,2,32,3072]{3,2,1,0:T(8,128)(2,1)} %param.14) | copy-start | bytes 1179652
  7.2 84.1 %all-gather.3.cloned.1.call-start = ((), (), s32[]{:S(2)}) async-start(), calls=%async_computation.2 | async-start | bytes 3538944 | tf_op jit(solution)/shard_map/all_gather | solution.py:9
  42.0 52.0 %copy-start.6 = (bf16[1,2,32,3072]{3,2,1,0:T(8,128)(2,1)S(1)}, bf16[1,2,32,3072]{3,2,1,0:T(8,128)(2,1)}, u32[]{:S(2)}) copy-start(bf16[1,2,32,3072]{3,2,1,0:T(8,128)(2,1)} %param.15) | copy-start | bytes 1179652
  91.3 2.8 copy-start.1
  97.3 8.8 %copy-start.8 = (s32[1,2,2048]{2,1,0:T(2,128)S(1)}, s32[1,2,2048]{2,1,0:T(2,128)}, u32[]{:S(2)}) copy-start(s32[1,2,2048]{2,1,0:T(2,128)} %param.16) | copy-start | bytes 49156
  97.3 103.9 %all-to-all-start = ((bf16[64,1,2,64,256]{4,3,2,1,0:T(8,128)(2,1)}), bf16[64,1,2,64,256]{4,3,2,1,0:T(8,128)(2,1)}, u32[]{:S(2)}, u32[]{:S(2)}) async-start(bf16[64,1,2,64,256]{4,3,2,1,0:T(8,128)(2,1)} %stack.4), calls=%async_computation | async-start | bytes 8388608 | tf_op jit(solution)/shard_map/all_to_all | solution.py:15
  106.0 201.0 %all-gather.5.cloned.1.call-start = ((), (), s32[]{:S(2)}) async-start(), calls=%async_computation.3 | async-start | bytes 2359296 | tf_op jit(solution)/shard_map/all_gather | solution.py:9
  205.5 28.5 %copy-start.7 = (bf16[1,512,256]{2,1,0:T(8,128)(2,1)S(1)}, bf16[1,512,256]{2,1,0:T(8,128)(2,1)}, u32[]{:S(2)}) copy-start(bf16[1,512,256]{2,1,0:T(8,128)(2,1)} %param.19) | copy-start | bytes 786436
  309.3 9.3 %copy-start.9 = (s32[1,2,2048]{2,1,0:T(2,128)S(1)}, s32[1,2,2048]{2,1,0:T(2,128)}, u32[]{:S(2)}) copy-start(s32[1,2,2048]{2,1,0:T(2,128)} %param.17) | copy-start | bytes 49156
  309.3 9.4 %copy-start.10 = (s32[1,2048]{1,0:T(1,128)S(1)}, s32[1,2048]{1,0:T(1,128)}, u32[]{:S(2)}) copy-start(s32[1,2048]{1,0:T(1,128)} %param.21) | copy-start | bytes 24580
  310.4 37.5 %all-to-all-start.1 = ((bf16[64,1,1,32,256]{4,3,2,1,0:T(8,128)(2,1)}), bf16[64,1,1,32,256]{4,3,2,1,0:T(8,128)(2,1)}, u32[]{:S(2)}, u32[]{:S(2)}) async-start(bf16[64,1,1,32,256]{4,3,2,1,0:T(8,128)(2,1)} %stack.5), calls=%async_computation.1 | async-start | bytes 2097152 | tf_op jit(solution)/shard_map/all_to_all | solution.py:15
  318.5 129.6 %all-reduce.5.cloned.1.call-start = ((), (), s32[]{:S(2)}) async-start(), calls=%async_computation.4 | async-start | bytes 2097152 | tf_op jit(solution)/shard_map/psum | solution.py:83
  347.9 14.9 %copy-start.2 = (f32[1025,256]{1,0:T(8,128)S(1)}, f32[1025,256]{1,0:T(8,128)}, u32[]{:S(2)}) copy-start(f32[1025,256]{1,0:T(8,128)} %scatter_custom_fusion.1) | copy-start | bytes 3148804
  362.9 1.2 copy-start.3
  362.9 85.2 %copy-start.4 = (bf16[1024,256]{1,0:T(8,128)(2,1)S(1)}, bf16[1024,256]{1,0:T(8,128)(2,1)}, u32[]{:S(2)}) copy-start(bf16[1024,256]{1,0:T(8,128)(2,1)} %param.23) | copy-start | bytes 1572868
Sparse Core Ops, SparseCore 0:
  42.2 49.0 all-gather.2
  268.7 38.1 all-gather.4
  364.2 83.8 all-reduce.4
